TPU v7x, 128 devices: a whole 4x4x4 slice. The times are simulated.
128 devices in a mesh: dp: 8 (over z_hi, y), ty: 4 (over z_lo, core), tz: 4 (over x).
Axes of the slice: x: 4, y: 4, z: 4 (z_hi: 2, z_lo: 2; z = z_hi * 2 + z_lo), core: 2. Of those that a mesh axis runs over, the one named last changes fastest.
Arguments:
- inputs: bfloat16 [8, 4, 48, 48, 256], P('dp', None, 'ty', 'tz'), may hold values from -6 to 6
- pre_first: bfloat16 [8, 4, 48, 48, 256], P('dp', None, 'ty', 'tz'), may hold values from -6 to 6
- pre_second: bfloat16 [8, 4, 48, 48, 256], P('dp', None, 'ty', 'tz'), may hold values from -6 to 6
- grad_out: bfloat16 [8, 4, 48, 48, 256], P('dp', None, 'ty', 'tz'), may hold values from -6 to 6
- w_first: bfloat16 [256, 27, 256], P('dp'), may hold values from -0.078125 to 0.078125
- w_second: bfloat16 [256, 27, 256], P('dp'), may hold values from -0.078125 to 0.078125
Outputs:
- grad_input: bfloat16 [8, 4, 48, 48, 256], P('dp', None, 'ty', 'tz')
- grad_w_first: float32 [256, 27, 256], P('dp')
- grad_w_second: float32 [256, 27, 256], P('dp')
All inputs are finite; a program needn't handle non-finite values.
Results may differ from a plain program's by a relative error of at most 0.0049.
Values may be sent and summed in bfloat16 or wider, within the bound.
No kernel may reach another device: no remote copies, remote signals or barrier semaphores. Data moves between devices by JAX's collectives and lax.ppermute only.
A program may use at most 128 MiB of HBM per device.

v0:
```python
import math
import jax
import jax.numpy as jnp
from jax import lax
from jax.sharding import PartitionSpec as P


def extended(block, sides, width):
    for axis, dim in sides:
        count = lax.axis_size(axis)
        forward = [(i, i + 1) for i in range(count - 1)]
        backward = [(target, source) for source, target in forward]
        low = lax.ppermute(
            lax.slice_in_dim(block, block.shape[dim] - width, None, axis=dim), axis, forward
        )
        high = lax.ppermute(lax.slice_in_dim(block, 0, width, axis=dim), axis, backward)
        block = jnp.concatenate([low, block, high], axis=dim)
    return block


def make_offsets():
    return [
        (shift_a, shift_b, shift_c)
        for shift_a in (-1, 0, 1)
        for shift_b in (-1, 0, 1)
        for shift_c in (-1, 0, 1)
    ]


def pad_depth(field):
    return jnp.pad(field, ((0, 0), (1, 1), (0, 0), (0, 0), (0, 0)))


def window(padded, offset, shape):
    return padded[
        :,
        1 + offset[0] : 1 + offset[0] + shape[1],
        1 + offset[1] : 1 + offset[1] + shape[2],
        1 + offset[2] : 1 + offset[2] + shape[3],
        :,
    ]


def transpose_maker(grad_pad, shape, piece):
    total = jnp.zeros((shape[0] * shape[1] * shape[2] * shape[3], piece.shape[0]), jnp.float32)
    for index, offset in enumerate(make_offsets()):
        back = (-offset[0], -offset[1], -offset[2])
        sliced = window(grad_pad, back, shape).reshape(-1, grad_pad.shape[4])
        total = total + lax.dot_general(
            sliced, piece[:, index, :], (((1,), (1,)), ((), ())), preferred_element_type=jnp.float32
        )
    return total.reshape(shape[0], shape[1], shape[2], shape[3], piece.shape[0])


def filter_from_inputs(act_pad, grad, shape):
    flat_grad = grad.reshape(-1, grad.shape[4])
    terms = []
    for index, offset in enumerate(make_offsets()):
        sliced = window(act_pad, offset, shape).reshape(-1, act_pad.shape[4])
        terms.append(
            lax.dot_general(
                sliced, flat_grad, (((0,), (0,)), ((), ())), preferred_element_type=jnp.float32
            )
        )
    return jnp.stack(terms, axis=1)


def reduce_terms(partial_value):
    ch_in, tap_count, ch_out = partial_value.shape
    flat = partial_value.reshape(ch_in * tap_count, ch_out)
    share = lax.psum_scatter(flat, ("dp", "ty", "tz"), scatter_dimension=0, tiled=True)
    whole = lax.all_gather(share, ("ty", "tz"), axis=0, tiled=True)
    return whole.reshape(-1, tap_count, ch_out)


def local(inputs, pre_first, pre_second, grad_out, w_first, w_second):
    shape = grad_out.shape
    count = (
        shape[0]
        * shape[1]
        * shape[2]
        * shape[3]
        * lax.axis_size("dp")
        * lax.axis_size("ty")
        * lax.axis_size("tz")
    )
    scale = 1.0 / math.sqrt(count)
    zero_half = jnp.zeros((), jnp.bfloat16)
    grad_top = jnp.where(pre_second > 0, grad_out, zero_half)
    active = jnp.where(pre_first > 0, pre_first, zero_half)
    top_pad = pad_depth(extended(grad_top, (("ty", 2), ("tz", 3)), 1))
    upstream = transpose_maker(top_pad, shape, lax.all_gather(w_second, "dp", axis=0, tiled=True))
    grad_low = jnp.where(pre_first > 0, upstream, jnp.zeros((), jnp.float32)).astype(jnp.bfloat16)
    low_pad = pad_depth(extended(grad_low, (("ty", 2), ("tz", 3)), 1))
    input_pad, active_pad = (
        extended(inputs, (("ty", 2), ("tz", 3)), 1),
        extended(active, (("ty", 2), ("tz", 3)), 1),
    )
    part_second = filter_from_inputs(pad_depth(active_pad), grad_top, shape)
    part_first = filter_from_inputs(pad_depth(input_pad), grad_low, shape)
    grad_w_second = reduce_terms(part_second * scale)
    grad_input = transpose_maker(
        low_pad, shape, lax.all_gather(w_first, "dp", axis=0, tiled=True)
    ).astype(jnp.bfloat16)
    grad_w_first = reduce_terms(part_first * scale)
    return (grad_input, grad_w_first, grad_w_second)


def solution(mesh):
    placed = (
        P("dp", None, "ty", "tz", None),
        P("dp", None, "ty", "tz", None),
        P("dp", None, "ty", "tz", None),
        P("dp", None, "ty", "tz", None),
        P("dp", None, None),
        P("dp", None, None),
    )
    return jax.shard_map(
        local,
        mesh=mesh,
        in_specs=placed,
        out_specs=(P("dp", None, "ty", "tz", None), P("dp", None, None), P("dp", None, None)),
        check_vma=False,
    )
```

profile of v0, /device:TPU:82, one launch (start us, length us, event | category | flops | bytes accessed | tf_op | source)
XLA Modules:
  0.0 719.6 jit_solution(10167780539327095880)
XLA Ops:
  13.9 4.4 collective-permute-start.8
  20.6 3.4 collective-permute-start.2
  24.0 2.4 collective-permute-start.3
  31.3 3.4 collective-permute-start.10
  34.7 3.0 collective-permute-start.11
  39.4 2.4 fusion.181
  43.8 1.8 reshape.475
  45.6 1.8 reshape.476
  47.4 1.8 reshape.477
  49.2 1.8 reshape.478
  51.0 1.8 reshape.479
  52.8 1.8 reshape.480
  54.6 1.8 reshape.481
  56.4 1.8 reshape.482
  58.2 1.8 reshape.483
  59.9 1.8 reshape.484
  61.7 1.8 reshape.486
  63.6 1.8 reshape.487
  65.3 1.8 reshape.489
  67.2 1.8 reshape.490
  68.9 1.8 reshape.492
  70.7 1.8 reshape.493
  73.8 2.3 select_maximum_fusion.4
  94.2 3.2 collective-permute-start.12
  114.7 3.4 broadcast_multiply_fusion.1
  118.9 10.7 %copy.44 = f32[256,27,256]{2,1,0:T(8,128)} copy(f32[256,27,256]{2,0,1:T(8,128)} %broadcast_multiply_fusion.1) | data formatting | bytes 14155776 | tf_op jit(solution)/shard_map/mul | solution.py:105
  129.6 8.5 %mul.15 = f32[6912,256]{1,0:T(8,128)} reshape(f32[256,27,256]{2,1,0:T(8,128)} %copy.44) | data formatting | bytes 14155776 | tf_op jit(solution)/shard_map/mul | solution.py:105
  138.1 5.2 collective-permute-start.4
  144.8 2.9 collective-permute-start.14
  147.7 3.0 collective-permute-start.15
  152.3 2.9 collective-permute-start.6
  155.1 3.0 collective-permute-start.7
  169.0 7.7 %copy.46 = f32[256,27,256]{2,1,0:T(8,128)} copy(f32[256,27,256]{2,0,1:T(8,128)S(1)} %broadcast_multiply_fusion) | data formatting | bytes 14155776 | tf_op jit(solution)/shard_map/mul | solution.py:101
  176.7 8.5 %mul.17 = f32[6912,256]{1,0:T(8,128)} reshape(f32[256,27,256]{2,1,0:T(8,128)} %copy.46) | data formatting | bytes 14155776 | tf_op jit(solution)/shard_map/mul | solution.py:101
  185.2 293.6 %fusion.179 = (f32[56,256]{1,0:T(8,128)}, f32[56,256]{1,0:T(8,128)}) fusion(f32[6912,256]{1,0:T(8,128)} %mul.15, f32[6912,256]{1,0:T(8,128)} %mul.17), kind=kCustom, calls=%all-reduce-scatter.2 | all-reduce-scatter fusion | flops 3670017 | bytes 14270464
  480.2 4.4 collective-permute-start.21
  484.6 8.4 %collective-permute-start.22 = (f32[56,256]{1,0:T(8,128)}, f32[56,256]{1,0:T(8,128)}, u32[]{:S(2)}, u32[]{:S(2)}) collective-permute-start(f32[56,256]{1,0:T(8,128)} %get-tuple-element.15), channel_id=1, source_target_pairs={{0,2},{1,3},{2,4},{3,5},{4,6},{5,7},{6,8},{7,9},{8,10},{9,11},{10,... | collective-permute-start | bytes 172040
  493.0 10.4 %collective-permute-start.23 = (f32[56,256]{1,0:T(8,128)}, f32[56,256]{1,0:T(8,128)}, u32[]{:S(2)}, u32[]{:S(2)}) collective-permute-start(f32[56,256]{1,0:T(8,128)} %get-tuple-element.15), channel_id=1, source_target_pairs={{0,3},{1,4},{2,5},{3,6},{4,7},{5,8},{6,9},{7,10},{8,11},{9,12},{10... | collective-permute-start | bytes 172040
  503.4 11.3 %collective-permute-start.24 = (f32[56,256]{1,0:T(8,128)}, f32[56,256]{1,0:T(8,128)}, u32[]{:S(2)}, u32[]{:S(2)}) collective-permute-start(f32[56,256]{1,0:T(8,128)} %get-tuple-element.15), channel_id=1, source_target_pairs={{0,4},{1,5},{2,6},{3,7},{4,8},{5,9},{6,10},{7,11},{8,12},{9,13},{1... | collective-permute-start | bytes 172040
  514.7 16.8 %collective-permute-start.25 = (f32[30,256]{1,0:T(8,128)}, f32[30,256]{1,0:T(8,128)}, u32[]{:S(2)}, u32[]{:S(2)}) collective-permute-start(f32[30,256]{1,0:T(8,128)} %slice.943), channel_id=1, source_target_pairs={{0,5},{1,6},{2,7},{3,8},{4,9},{5,10},{6,11},{7,12},{8,13},{9,14},{... | collective-permute-start | bytes 92168
  531.9 2.5 fusion.180
  534.4 1.8 reshape.503
  536.2 1.8 reshape.504
  538.0 1.8 reshape.505
  541.5 1.8 reshape.507
  543.3 1.8 reshape.508
  545.1 1.8 reshape.509
  546.9 1.8 reshape.510
  551.7 1.8 reshape.512
  554.6 1.8 reshape.514
  556.3 1.8 reshape.515
  558.1 1.8 reshape.517
  560.7 1.8 reshape.520
  562.5 1.8 reshape.521
  564.2 1.8 reshape.522
  566.0 1.8 reshape.523
  587.4 3.5 collective-permute-start.16
  590.9 8.7 %collective-permute-start.17 = (f32[56,256]{1,0:T(8,128)S(1)}, f32[56,256]{1,0:T(8,128)S(1)}, u32[]{:S(2)}, u32[]{:S(2)}) collective-permute-start(f32[56,256]{1,0:T(8,128)S(1)} %copy-done.41), channel_id=1, source_target_pairs={{0,2},{1,3},{2,4},{3,5},{4,6},{5,7},{6,8},{7,9},{8,10},{9,11},{10,... | collective-permute-start | bytes 172040
  599.6 8.4 %collective-permute-start.18 = (f32[56,256]{1,0:T(8,128)S(1)}, f32[56,256]{1,0:T(8,128)S(1)}, u32[]{:S(2)}, u32[]{:S(2)}) collective-permute-start(f32[56,256]{1,0:T(8,128)S(1)} %copy-done.41), channel_id=1, source_target_pairs={{0,3},{1,4},{2,5},{3,6},{4,7},{5,8},{6,9},{7,10},{8,11},{9,12},{10... | collective-permute-start | bytes 172040
  608.0 14.2 %collective-permute-start.19 = (f32[56,256]{1,0:T(8,128)S(1)}, f32[56,256]{1,0:T(8,128)S(1)}, u32[]{:S(2)}, u32[]{:S(2)}) collective-permute-start(f32[56,256]{1,0:T(8,128)S(1)} %copy-done.41), channel_id=1, source_target_pairs={{0,4},{1,5},{2,6},{3,7},{4,8},{5,9},{6,10},{7,11},{8,12},{9,13},{1... | collective-permute-start | bytes 172040
  622.3 14.3 %collective-permute-start.20 = (f32[30,256]{1,0:T(8,128)S(1)}, f32[30,256]{1,0:T(8,128)S(1)}, u32[]{:S(2)}, u32[]{:S(2)}) collective-permute-start(f32[30,256]{1,0:T(8,128)S(1)} %slice.942), channel_id=1, source_target_pairs={{0,5},{1,6},{2,7},{3,8},{4,9},{5,10},{6,11},{7,12},{8,13},{9,14},{... | collective-permute-start | bytes 92168
  636.5 5.1 concatenate.113
  641.7 31.1 %all-gather.1 = f32[16,54,256]{2,1,0:T(8,128)S(1)} all-gather(f32[1,54,256]{2,1,0:T(8,128)S(1)} %dynamic-slice_bitcast_fusion), channel_id=1, replica_groups=mesh['dp'=8,'ty'=4,'tz'=4] {'ty','tz'}, dimensions={0}, use_global_device_ids=true | all-gather | bytes 940032 | tf_op jit(solution)/shard_map/all_gather | solution.py:72
  675.2 35.9 %all-gather = f32[16,54,256]{2,1,0:T(8,128)S(1)} all-gather(f32[1,54,256]{2,1,0:T(8,128)S(1)} %dynamic-slice_bitcast_fusion.1), channel_id=1, replica_groups=mesh['dp'=8,'ty'=4,'tz'=4] {'ty','tz'}, dimensions={0}, use_global_device_ids=true | all-gather | bytes 940032 | tf_op jit(solution)/shard_map/all_gather | solution.py:72
  (312 shorter events, 98.9 us)
Async XLA Ops:
  7.2 68.9 %all-gather.5.cloned.1.call-start = ((), (), s32[]{:S(2)}) async-start(), calls=%async_computation | async-start | bytes 3981312 | tf_op jit(solution)/shard_map/all_gather | solution.py:92
  7.9 562.6 %all-gather.7.cloned.1.call-start = ((), (), s32[]{:S(2)}) async-start(), calls=%async_computation.1 | async-start | bytes 3981312 | tf_op jit(solution)/shard_map/all_gather | solution.py:103
  9.1 11.4 %collective-permute-start = (bf16[1,4,1,12,256]{4,3,2,1,0:T(8,128)(2,1)S(1)}, bf16[1,4,1,12,256]{4,3,2,1,0:T(8,128)(2,1)S(1)}, u32[]{:S(2)}, u32[]{:S(2)}) collective-permute-start(bf16[1,4,1,12,256]{4,3,2,1,0:T(8,128)(2,1)S(1)} %get-tuple-element.88), channel_id=1, source_target_pairs={{0,4},{4,8},{8,12},{1,5},{5,9},{9,13},{2,6},{6,10},{10,14},{3,7},{... | collective-permute-start | bytes 73736 | tf_op jit(solution)/shard_map/ppermute | solution.py:13
  10.9 9.6 %collective-permute-start.1 = (bf16[1,4,1,12,256]{4,3,2,1,0:T(8,128)(2,1)S(1)}, bf16[1,4,1,12,256]{4,3,2,1,0:T(8,128)(2,1)S(1)}, u32[]{:S(2)}, u32[]{:S(2)}) collective-permute-start(bf16[1,4,1,12,256]{4,3,2,1,0:T(8,128)(2,1)S(1)} %get-tuple-element.89), channel_id=1, source_target_pairs={{4,0},{8,4},{12,8},{5,1},{9,5},{13,9},{6,2},{10,6},{14,10},{7,3},{... | collective-permute-start | bytes 73736 | tf_op jit(solution)/shard_map/ppermute | solution.py:16
  13.9 12.5 %collective-permute-start.8 = (bf16[1,4,1,12,256]{4,3,2,1,0:T(8,128)(2,1)S(1)}, bf16[1,4,1,12,256]{4,3,2,1,0:T(8,128)(2,1)S(1)}, u32[]{:S(2)}, u32[]{:S(2)}) collective-permute-start(bf16[1,4,1,12,256]{4,3,2,1,0:T(8,128)(2,1)S(1)} %get-tuple-element.81), channel_id=1, source_target_pairs={{0,4},{4,8},{8,12},{1,5},{5,9},{9,13},{2,6},{6,10},{10,14},{3,7},{... | collective-permute-start | bytes 73736 | tf_op jit(solution)/shard_map/ppermute | solution.py:13
  18.4 9.2 %collective-permute-start.9 = (bf16[1,4,1,12,256]{4,3,2,1,0:T(8,128)(2,1)S(1)}, bf16[1,4,1,12,256]{4,3,2,1,0:T(8,128)(2,1)S(1)}, u32[]{:S(2)}, u32[]{:S(2)}) collective-permute-start(bf16[1,4,1,12,256]{4,3,2,1,0:T(8,128)(2,1)S(1)} %get-tuple-element.80), channel_id=1, source_target_pairs={{4,0},{8,4},{12,8},{5,1},{9,5},{13,9},{6,2},{10,6},{14,10},{7,3},{... | collective-permute-start | bytes 73736 | tf_op jit(solution)/shard_map/ppermute | solution.py:16
  20.5 17.3 %copy-start.37 = (bf16[1,4,1,12,256]{4,3,2,1,0:T(8,128)(2,1)}, bf16[1,4,1,12,256]{4,3,2,1,0:T(8,128)(2,1)S(1)}, u32[]{:S(2)}) copy-start(bf16[1,4,1,12,256]{4,3,2,1,0:T(8,128)(2,1)S(1)} %collective-permute-done) | copy-start | bytes 73732
  20.5 17.3 %copy-start.39 = (bf16[1,4,1,12,256]{4,3,2,1,0:T(8,128)(2,1)}, bf16[1,4,1,12,256]{4,3,2,1,0:T(8,128)(2,1)S(1)}, u32[]{:S(2)}) copy-start(bf16[1,4,1,12,256]{4,3,2,1,0:T(8,128)(2,1)S(1)} %collective-permute-done.1) | copy-start | bytes 73732
  20.6 17.1 %collective-permute-start.2 = (bf16[1,4,14,1,256]{4,3,2,1,0:T(2,128)(2,1)S(1)}, bf16[1,4,14,1,256]{4,3,2,1,0:T(2,128)(2,1)S(1)}, u32[]{:S(2)}, u32[]{:S(2)}) collective-permute-start(bf16[1,4,14,1,256]{4,3,2,1,0:T(2,128)(2,1)S(1)} %get-tuple-element.77), channel_id=1, source_target_pairs={{0,1},{1,2},{2,3},{4,5},{5,6},{6,7},{8,9},{9,10},{10,11},{12,13},{... | collective-permute-start | bytes 86024 | tf_op jit(solution)/shard_map/ppermute | solution.py:13
  24.0 13.7 %collective-permute-start.3 = (bf16[1,4,14,1,256]{4,3,2,1,0:T(2,128)(2,1)S(1)}, bf16[1,4,14,1,256]{4,3,2,1,0:T(2,128)(2,1)S(1)}, u32[]{:S(2)}, u32[]{:S(2)}) collective-permute-start(bf16[1,4,14,1,256]{4,3,2,1,0:T(2,128)(2,1)S(1)} %get-tuple-element.76), channel_id=1, source_target_pairs={{1,0},{2,1},{3,2},{5,4},{6,5},{7,6},{9,8},{10,9},{11,10},{13,12},{... | collective-permute-start | bytes 86024 | tf_op jit(solution)/shard_map/ppermute | solution.py:16
  31.3 42.5 %collective-permute-start.10 = (bf16[1,4,14,1,256]{4,3,2,1,0:T(2,128)(2,1)}, bf16[1,4,14,1,256]{4,3,2,1,0:T(2,128)(2,1)}, u32[]{:S(2)}, u32[]{:S(2)}) collective-permute-start(bf16[1,4,14,1,256]{4,3,2,1,0:T(2,128)(2,1)} %get-tuple-element.56), channel_id=1, source_target_pairs={{0,1},{1,2},{2,3},{4,5},{5,6},{6,7},{8,9},{9,10},{10,11},{12,13},{... | collective-permute-start | bytes 86024 | tf_op jit(solution)/shard_map/ppermute | solution.py:13
  34.7 39.1 %collective-permute-start.11 = (bf16[1,4,14,1,256]{4,3,2,1,0:T(2,128)(2,1)}, bf16[1,4,14,1,256]{4,3,2,1,0:T(2,128)(2,1)}, u32[]{:S(2)}, u32[]{:S(2)}) collective-permute-start(bf16[1,4,14,1,256]{4,3,2,1,0:T(2,128)(2,1)} %get-tuple-element.57), channel_id=1, source_target_pairs={{1,0},{2,1},{3,2},{5,4},{6,5},{7,6},{9,8},{10,9},{11,10},{13,12},{... | collective-permute-start | bytes 86024 | tf_op jit(solution)/shard_map/ppermute | solution.py:16
  39.4 2.5 copy-start.38
  39.4 2.5 copy-start.40
  39.4 2.5 copy-start.46
  39.4 2.5 copy-start.48
  73.8 8.9 %copy-start.30 = (bf16[576,256]{1,0:T(8,128)(2,1)S(1)}, bf16[576,256]{1,0:T(8,128)(2,1)}, u32[]{:S(2)}) copy-start(bf16[576,256]{1,0:T(8,128)(2,1)} %reshape.478) | copy-start | bytes 884740
  76.1 7.8 %copy-start.1 = (bf16[256,27,256]{2,0,1:T(8,128)(2,1)S(1)}, bf16[256,27,256]{2,0,1:T(8,128)(2,1)}, u32[]{:S(2)}) copy-start(bf16[256,27,256]{2,0,1:T(8,128)(2,1)} %all-gather.5.cloned.1.call-done) | copy-start | bytes 10616836
  76.1 7.8 %copy-start.28 = (bf16[576,256]{1,0:T(8,128)(2,1)S(1)}, bf16[576,256]{1,0:T(8,128)(2,1)}, u32[]{:S(2)}) copy-start(bf16[576,256]{1,0:T(8,128)(2,1)} %reshape.479) | copy-start | bytes 884740
  76.1 12.0 %copy-start.24 = (bf16[576,256]{1,0:T(8,128)(2,1)S(1)}, bf16[576,256]{1,0:T(8,128)(2,1)}, u32[]{:S(2)}) copy-start(bf16[576,256]{1,0:T(8,128)(2,1)} %reshape.483) | copy-start | bytes 884740
  78.8 9.6 %copy-start.23 = (bf16[576,256]{1,0:T(8,128)(2,1)S(1)}, bf16[576,256]{1,0:T(8,128)(2,1)}, u32[]{:S(2)}) copy-start(bf16[576,256]{1,0:T(8,128)(2,1)} %reshape.484) | copy-start | bytes 884740
  80.1 8.6 %copy-start.4 = (bf16[576,256]{1,0:T(8,128)(2,1)S(1)}, bf16[576,256]{1,0:T(8,128)(2,1)}, u32[]{:S(2)}) copy-start(bf16[576,256]{1,0:T(8,128)(2,1)} %reshape.485) | copy-start | bytes 884740
  82.7 6.3 copy-start.19
  83.9 5.3 copy-start.7
  84.2 5.3 copy-start.14
  85.5 4.3 copy-start.12
  86.8 3.3 copy-start.3
  91.8 8.7 %copy-start.33 = (bf16[1,6,14,14,256]{4,3,2,1,0:T(8,128)(2,1)S(1)}, bf16[1,6,14,14,256]{4,3,2,1,0:T(8,128)(2,1)}, u32[]{:S(2)}) copy-start(bf16[1,6,14,14,256]{4,3,2,1,0:T(8,128)(2,1)} %select_maximum_fusion.4) | copy-start | bytes 1806340
  94.2 50.5 %collective-permute-start.12 = (bf16[1,4,1,12,256]{4,3,2,1,0:T(8,128)(2,1)S(1)}, bf16[1,4,1,12,256]{4,3,2,1,0:T(8,128)(2,1)S(1)}, u32[]{:S(2)}, u32[]{:S(2)}) collective-permute-start(bf16[1,4,1,12,256]{4,3,2,1,0:T(8,128)(2,1)S(1)} %get-tuple-element.78), channel_id=1, source_target_pairs={{0,4},{4,8},{8,12},{1,5},{5,9},{9,13},{2,6},{6,10},{10,14},{3,7},{... | collective-permute-start | bytes 73736 | tf_op jit(solution)/shard_map/ppermute | solution.py:13
  97.4 47.2 %collective-permute-start.13 = (bf16[1,4,1,12,256]{4,3,2,1,0:T(8,128)(2,1)S(1)}, bf16[1,4,1,12,256]{4,3,2,1,0:T(8,128)(2,1)S(1)}, u32[]{:S(2)}, u32[]{:S(2)}) collective-permute-start(bf16[1,4,1,12,256]{4,3,2,1,0:T(8,128)(2,1)S(1)} %get-tuple-element.79), channel_id=1, source_target_pairs={{4,0},{8,4},{12,8},{5,1},{9,5},{13,9},{6,2},{10,6},{14,10},{7,3},{... | collective-permute-start | bytes 73736 | tf_op jit(solution)/shard_map/ppermute | solution.py:16
  105.0 2.5 copy-start.5
  107.5 2.7 copy-start.50
  138.1 12.5 %collective-permute-start.4 = (bf16[1,4,1,12,256]{4,3,2,1,0:T(8,128)(2,1)S(1)}, bf16[1,4,1,12,256]{4,3,2,1,0:T(8,128)(2,1)S(1)}, u32[]{:S(2)}, u32[]{:S(2)}) collective-permute-start(bf16[1,4,1,12,256]{4,3,2,1,0:T(8,128)(2,1)S(1)} %get-tuple-element.84), channel_id=1, source_target_pairs={{0,4},{4,8},{8,12},{1,5},{5,9},{9,13},{2,6},{6,10},{10,14},{3,7},{... | collective-permute-start | bytes 73736 | tf_op jit(solution)/shard_map/ppermute | solution.py:13
  143.3 7.3 %collective-permute-start.5 = (bf16[1,4,1,12,256]{4,3,2,1,0:T(8,128)(2,1)S(1)}, bf16[1,4,1,12,256]{4,3,2,1,0:T(8,128)(2,1)S(1)}, u32[]{:S(2)}, u32[]{:S(2)}) collective-permute-start(bf16[1,4,1,12,256]{4,3,2,1,0:T(8,128)(2,1)S(1)} %get-tuple-element.85), channel_id=1, source_target_pairs={{4,0},{8,4},{12,8},{5,1},{9,5},{13,9},{6,2},{10,6},{14,10},{7,3},{... | collective-permute-start | bytes 73736 | tf_op jit(solution)/shard_map/ppermute | solution.py:16
  144.8 13.4 %collective-permute-start.14 = (bf16[1,4,14,1,256]{4,3,2,1,0:T(2,128)(2,1)S(1)}, bf16[1,4,14,1,256]{4,3,2,1,0:T(2,128)(2,1)S(1)}, u32[]{:S(2)}, u32[]{:S(2)}) collective-permute-start(bf16[1,4,14,1,256]{4,3,2,1,0:T(2,128)(2,1)S(1)} %get-tuple-element.54), channel_id=1, source_target_pairs={{0,1},{1,2},{2,3},{4,5},{5,6},{6,7},{8,9},{9,10},{10,11},{12,13},{... | collective-permute-start | bytes 86024 | tf_op jit(solution)/shard_map/ppermute | solution.py:13
  147.7 10.5 %collective-permute-start.15 = (bf16[1,4,14,1,256]{4,3,2,1,0:T(2,128)(2,1)S(1)}, bf16[1,4,14,1,256]{4,3,2,1,0:T(2,128)(2,1)S(1)}, u32[]{:S(2)}, u32[]{:S(2)}) collective-permute-start(bf16[1,4,14,1,256]{4,3,2,1,0:T(2,128)(2,1)S(1)} %get-tuple-element.55), channel_id=1, source_target_pairs={{1,0},{2,1},{3,2},{5,4},{6,5},{7,6},{9,8},{10,9},{11,10},{13,12},{... | collective-permute-start | bytes 86024 | tf_op jit(solution)/shard_map/ppermute | solution.py:16
  150.6 380.8 %copy-start.36 = (bf16[1,4,1,12,256]{4,3,2,1,0:T(8,128)(2,1)}, bf16[1,4,1,12,256]{4,3,2,1,0:T(8,128)(2,1)S(1)}, u32[]{:S(2)}) copy-start(bf16[1,4,1,12,256]{4,3,2,1,0:T(8,128)(2,1)S(1)} %collective-permute-done.5) | copy-start | bytes 73732
  152.3 351.1 %collective-permute-start.6 = (bf16[1,4,14,1,256]{4,3,2,1,0:T(2,128)(2,1)}, bf16[1,4,14,1,256]{4,3,2,1,0:T(2,128)(2,1)S(1)}, u32[]{:S(2)}, u32[]{:S(2)}) collective-permute-start(bf16[1,4,14,1,256]{4,3,2,1,0:T(2,128)(2,1)} %get-tuple-element.67), channel_id=1, source_target_pairs={{0,1},{1,2},{2,3},{4,5},{5,6},{6,7},{8,9},{9,10},{10,11},{12,13},{... | collective-permute-start | bytes 86024 | tf_op jit(solution)/shard_map/ppermute | solution.py:13
  155.1 359.5 %collective-permute-start.7 = (bf16[1,4,14,1,256]{4,3,2,1,0:T(2,128)(2,1)}, bf16[1,4,14,1,256]{4,3,2,1,0:T(2,128)(2,1)S(1)}, u32[]{:S(2)}, u32[]{:S(2)}) collective-permute-start(bf16[1,4,14,1,256]{4,3,2,1,0:T(2,128)(2,1)} %get-tuple-element.66), channel_id=1, source_target_pairs={{1,0},{2,1},{3,2},{5,4},{6,5},{7,6},{9,8},{10,9},{11,10},{13,12},{... | collective-permute-start | bytes 86024 | tf_op jit(solution)/shard_map/ppermute | solution.py:16
  480.2 110.7 %collective-permute-start.21 = (f32[56,256]{1,0:T(8,128)}, f32[56,256]{1,0:T(8,128)}, u32[]{:S(2)}, u32[]{:S(2)}) collective-permute-start(f32[56,256]{1,0:T(8,128)} %get-tuple-element.15), channel_id=1, source_target_pairs={{0,1},{1,2},{2,3},{3,4},{4,5},{5,6},{6,7},{7,8},{8,9},{9,10},{10,1... | collective-permute-start | bytes 172040
  484.6 115.1 %collective-permute-start.22 = (f32[56,256]{1,0:T(8,128)}, f32[56,256]{1,0:T(8,128)}, u32[]{:S(2)}, u32[]{:S(2)}) collective-permute-start(f32[56,256]{1,0:T(8,128)} %get-tuple-element.15), channel_id=1, source_target_pairs={{0,2},{1,3},{2,4},{3,5},{4,6},{5,7},{6,8},{7,9},{8,10},{9,11},{10,... | collective-permute-start | bytes 172040
  493.0 115.1 %collective-permute-start.23 = (f32[56,256]{1,0:T(8,128)}, f32[56,256]{1,0:T(8,128)}, u32[]{:S(2)}, u32[]{:S(2)}) collective-permute-start(f32[56,256]{1,0:T(8,128)} %get-tuple-element.15), channel_id=1, source_target_pairs={{0,3},{1,4},{2,5},{3,6},{4,7},{5,8},{6,9},{7,10},{8,11},{9,12},{10... | collective-permute-start | bytes 172040
  503.4 28.1 %copy-start.43 = (bf16[1,4,14,1,256]{4,3,2,1,0:T(2,128)(2,1)}, bf16[1,4,14,1,256]{4,3,2,1,0:T(2,128)(2,1)S(1)}, u32[]{:S(2)}) copy-start(bf16[1,4,14,1,256]{4,3,2,1,0:T(2,128)(2,1)S(1)} %collective-permute-done.6) | copy-start | bytes 86020
  503.4 118.9 %collective-permute-start.24 = (f32[56,256]{1,0:T(8,128)}, f32[56,256]{1,0:T(8,128)}, u32[]{:S(2)}, u32[]{:S(2)}) collective-permute-start(f32[56,256]{1,0:T(8,128)} %get-tuple-element.15), channel_id=1, source_target_pairs={{0,4},{1,5},{2,6},{3,7},{4,8},{5,9},{6,10},{7,11},{8,12},{9,13},{1... | collective-permute-start | bytes 172040
  514.7 16.9 %copy-start.44 = (bf16[1,4,14,1,256]{4,3,2,1,0:T(2,128)(2,1)}, bf16[1,4,14,1,256]{4,3,2,1,0:T(2,128)(2,1)S(1)}, u32[]{:S(2)}) copy-start(bf16[1,4,14,1,256]{4,3,2,1,0:T(2,128)(2,1)S(1)} %collective-permute-done.7) | copy-start | bytes 86020
  514.7 72.7 %collective-permute-start.25 = (f32[30,256]{1,0:T(8,128)}, f32[30,256]{1,0:T(8,128)}, u32[]{:S(2)}, u32[]{:S(2)}) collective-permute-start(f32[30,256]{1,0:T(8,128)} %slice.943), channel_id=1, source_target_pairs={{0,5},{1,6},{2,7},{3,8},{4,9},{5,10},{6,11},{7,12},{8,13},{9,14},{... | collective-permute-start | bytes 92168
  559.9 17.2 %copy-start.16 = (bf16[576,256]{1,0:T(8,128)(2,1)S(1)}, bf16[576,256]{1,0:T(8,128)(2,1)}, u32[]{:S(2)}) copy-start(bf16[576,256]{1,0:T(8,128)(2,1)} %reshape.506) | copy-start | bytes 884740
  569.4 11.5 %copy-start.13 = (bf16[576,256]{1,0:T(8,128)(2,1)S(1)}, bf16[576,256]{1,0:T(8,128)(2,1)}, u32[]{:S(2)}) copy-start(bf16[576,256]{1,0:T(8,128)(2,1)} %reshape.509) | copy-start | bytes 884740
  570.3 10.9 %copy-start.11 = (bf16[576,256]{1,0:T(8,128)(2,1)S(1)}, bf16[576,256]{1,0:T(8,128)(2,1)}, u32[]{:S(2)}) copy-start(bf16[576,256]{1,0:T(8,128)(2,1)} %reshape.510) | copy-start | bytes 884740
  570.4 11.1 %copy-start.10 = (bf16[576,256]{1,0:T(8,128)(2,1)S(1)}, bf16[576,256]{1,0:T(8,128)(2,1)}, u32[]{:S(2)}) copy-start(bf16[576,256]{1,0:T(8,128)(2,1)} %reshape.511) | copy-start | bytes 884740
  570.5 7.8 %copy-start = (bf16[256,27,256]{2,0,1:T(8,128)(2,1)S(1)}, bf16[256,27,256]{2,0,1:T(8,128)(2,1)}, u32[]{:S(2)}) copy-start(bf16[256,27,256]{2,0,1:T(8,128)(2,1)} %all-gather.7.cloned.1.call-done) | copy-start | bytes 10616836
  573.2 8.6 %copy-start.27 = (bf16[576,256]{1,0:T(8,128)(2,1)S(1)}, bf16[576,256]{1,0:T(8,128)(2,1)}, u32[]{:S(2)}) copy-start(bf16[576,256]{1,0:T(8,128)(2,1)} %reshape.512) | copy-start | bytes 884740
  574.5 7.6 %copy-start.2 = (bf16[576,256]{1,0:T(8,128)(2,1)S(1)}, bf16[576,256]{1,0:T(8,128)(2,1)}, u32[]{:S(2)}) copy-start(bf16[576,256]{1,0:T(8,128)(2,1)} %reshape.513) | copy-start | bytes 884740
  577.1 5.3 copy-start.29
  578.3 4.4 copy-start.6
  579.6 3.4 copy-start.25
  580.9 2.4 copy-start.26
  581.8 2.3 copy-start.21
  583.8 2.5 copy-start.41
  587.4 86.9 %collective-permute-start.16 = (f32[56,256]{1,0:T(8,128)S(1)}, f32[56,256]{1,0:T(8,128)S(1)}, u32[]{:S(2)}, u32[]{:S(2)}) collective-permute-start(f32[56,256]{1,0:T(8,128)S(1)} %copy-done.41), channel_id=1, source_target_pairs={{0,1},{1,2},{2,3},{3,4},{4,5},{5,6},{6,7},{7,8},{8,9},{9,10},{10,1... | collective-permute-start | bytes 172040
  590.9 83.4 %collective-permute-start.17 = (f32[56,256]{1,0:T(8,128)S(1)}, f32[56,256]{1,0:T(8,128)S(1)}, u32[]{:S(2)}, u32[]{:S(2)}) collective-permute-start(f32[56,256]{1,0:T(8,128)S(1)} %copy-done.41), channel_id=1, source_target_pairs={{0,2},{1,3},{2,4},{3,5},{4,6},{5,7},{6,8},{7,9},{8,10},{9,11},{10,... | collective-permute-start | bytes 172040
  599.6 74.7 %collective-permute-start.18 = (f32[56,256]{1,0:T(8,128)S(1)}, f32[56,256]{1,0:T(8,128)S(1)}, u32[]{:S(2)}, u32[]{:S(2)}) collective-permute-start(f32[56,256]{1,0:T(8,128)S(1)} %copy-done.41), channel_id=1, source_target_pairs={{0,3},{1,4},{2,5},{3,6},{4,7},{5,8},{6,9},{7,10},{8,11},{9,12},{10... | collective-permute-start | bytes 172040
  608.0 66.3 %collective-permute-start.19 = (f32[56,256]{1,0:T(8,128)S(1)}, f32[56,256]{1,0:T(8,128)S(1)}, u32[]{:S(2)}, u32[]{:S(2)}) collective-permute-start(f32[56,256]{1,0:T(8,128)S(1)} %copy-done.41), channel_id=1, source_target_pairs={{0,4},{1,5},{2,6},{3,7},{4,8},{5,9},{6,10},{7,11},{8,12},{9,13},{1... | collective-permute-start | bytes 172040
  622.3 52.0 %collective-permute-start.20 = (f32[30,256]{1,0:T(8,128)S(1)}, f32[30,256]{1,0:T(8,128)S(1)}, u32[]{:S(2)}, u32[]{:S(2)}) collective-permute-start(f32[30,256]{1,0:T(8,128)S(1)} %slice.942), channel_id=1, source_target_pairs={{0,5},{1,6},{2,7},{3,8},{4,9},{5,10},{6,11},{7,12},{8,13},{9,14},{... | collective-permute-start | bytes 92168
  (17 other events, 26.3 us)
Sparse Core Ops, SparseCore 0:
  10.3 63.1 all-gather.4
  75.9 64.0 all-gather.6
where the time goes:
time: 731 us; the launch traced here: 720 us
  blocking collectives  361 us (49%)
  starting transfers between devices  145 us (20%)
  local copies, waits for them, and re-layouts  129 us (18%)
  matrix products  55.2 us (8%)
  between operations  16.4 us (2%)
  other arithmetic  13.1 us (2%)
    unnamed x1, blocking collectives  294 us
    unnamed x10, starting transfers between devices  100 us
    all_gather x2, blocking collectives, reduce_terms(): whole = lax.all_gather(share, ('ty', 'tz'), axis=0, tiled=True)  66.9 us
    reshape x54, local copies, waits for them, and re-layouts, transpose_maker(): sliced = window(grad_pad, back, shape).reshape(-1, grad_pad.shape[4])  66.5 us
    dot_general x54, matrix products, transpose_maker(): lax.dot_general(sliced, piece[:, index, :], (((1,), (1,)), ((), ())), pre...  31.8 us
    ppermute x8, starting transfers between devices, extended(): lax.ppermute(lax.slice_in_dim(block, block.shape[dim] - width, None, axis...  27.1 us
    dot_general x54, matrix products, filter_from_inputs(): lax.dot_general(sliced, flat_grad, (((0,), (0,)), ((), ())), preferred_el...  23.5 us
    mul x2, local copies, waits for them, and re-layouts, local(): grad_w_first = reduce_terms(part_first * scale)  19.2 us
  transfers between devices with their start and end apart: 28, of which 0 were waited for; matrix products, arithmetic and copies ran while one was open for 67% of the time, Pallas kernels for 0%

commit v1 on v0

--- a/solution.py
+++ b/solution.py
@@ -69,7 +69,9 @@
     ch_in, tap_count, ch_out = partial_value.shape
     flat = partial_value.reshape(ch_in * tap_count, ch_out)
     share = lax.psum_scatter(flat, ("dp", "ty", "tz"), scatter_dimension=0, tiled=True)
-    whole = lax.all_gather(share, ("ty", "tz"), axis=0, tiled=True)
+    whole = jnp.concatenate(
+        lax.all_to_all(jnp.stack([share] * lax.axis_size(("ty", "tz"))), ("ty", "tz"), 0, 0), axis=0
+    )
     return whole.reshape(-1, tap_count, ch_out)
 
 

time: 731 us -> 689 us (0.943)
  blocking collectives: 361 us -> 294 us
  waiting for transfers between devices: 0.79 us -> 12.1 us
  starting transfers between devices: 145 us -> 154 us
    all_gather x2 -> x0, blocking collectives: 66.9 us -> none  [reduce_terms(): whole = lax.all_gather(share, ('ty', 'tz'), axis=0, tiled=True)]
    all_to_all x0 -> x2, waiting for transfers between devices: none -> 11.3 us  [reduce_terms(): lax.all_to_all(jnp.stack([share] * lax.axis_size(('ty', 'tz'))), ('ty', '...]
    all_to_all x0 -> x2, starting transfers between devices: none -> 9.14 us  [reduce_terms(): lax.all_to_all(jnp.stack([share] * lax.axis_size(('ty', 'tz'))), ('ty', '...]
  transfers between devices with their start and end apart: 28 -> 30, of which waited for: 0 -> 2; matrix products, arithmetic and copies ran while one was open for 67% -> 72% of each run, Pallas kernels for 0% -> 0%
where the time goes in v1:
time: 689 us; the launch traced here: 677 us
  blocking collectives  294 us (43%)
  starting transfers between devices  154 us (22%)
  local copies, waits for them, and re-layouts  129 us (19%)
  matrix products  59.8 us (9%)
  between operations  16.5 us (2%)
  other arithmetic  12.4 us (2%)
  waiting for transfers between devices  12.1 us (2%)
    unnamed x1, blocking collectives  294 us
    unnamed x10, starting transfers between devices  100 us
    reshape x54, local copies, waits for them, and re-layouts, transpose_maker(): sliced = window(grad_pad, back, shape).reshape(-1, grad_pad.shape[4])  64.1 us
    dot_general x54, matrix products, transpose_maker(): lax.dot_general(sliced, piece[:, index, :], (((1,), (1,)), ((), ())), pre...  36.4 us
    ppermute x8, starting transfers between devices, extended(): lax.ppermute(lax.slice_in_dim(block, block.shape[dim] - width, None, axis...  27.1 us
    dot_general x54, matrix products, filter_from_inputs(): lax.dot_general(sliced, flat_grad, (((0,), (0,)), ((), ())), preferred_el...  23.5 us
    mul x2, local copies, waits for them, and re-layouts, local(): grad_w_first = reduce_terms(part_first * scale)  19.2 us
    unnamed x118, local copies, waits for them, and re-layouts  17.9 us
  transfers between devices with their start and end apart: 30, of which 2 were waited for; matrix products, arithmetic and copies ran while one was open for 72% of the time, Pallas kernels for 0%

profile of v1, /device:TPU:82, one launch (start us, length us, event | category | flops | bytes accessed | tf_op | source)
XLA Modules:
  0.0 677.2 jit_solution(12183429948409983282)
XLA Ops:
  14.0 4.4 collective-permute-start.8
  20.6 3.4 collective-permute-start.2
  24.0 2.4 collective-permute-start.3
  31.3 3.4 collective-permute-start.10
  34.7 3.1 collective-permute-start.11
  39.4 2.4 fusion.181
  43.8 1.8 reshape.473
  45.6 1.8 reshape.474
  47.4 1.8 reshape.475
  49.2 1.8 reshape.476
  51.0 1.8 reshape.477
  52.8 1.8 reshape.478
  54.5 1.8 reshape.479
  56.3 1.8 reshape.480
  58.2 1.8 reshape.481
  59.9 1.8 reshape.482
  61.7 1.8 reshape.484
  63.5 1.8 reshape.485
  65.3 1.8 reshape.487
  67.1 1.8 reshape.488
  68.9 1.8 reshape.490
  70.6 1.8 reshape.491
  73.8 2.3 select_maximum_fusion.4
  94.1 3.2 collective-permute-start.12
  97.3 1.8 collective-permute-start.13
  114.7 3.4 broadcast_multiply_fusion.1
  118.9 10.7 %copy.44 = f32[256,27,256]{2,1,0:T(8,128)} copy(f32[256,27,256]{2,0,1:T(8,128)} %broadcast_multiply_fusion.1) | data formatting | bytes 14155776 | tf_op jit(solution)/shard_map/mul | solution.py:107
  129.6 8.5 %mul.15 = f32[6912,256]{1,0:T(8,128)} reshape(f32[256,27,256]{2,1,0:T(8,128)} %copy.44) | data formatting | bytes 14155776 | tf_op jit(solution)/shard_map/mul | solution.py:107
  138.1 5.3 collective-permute-start.4
  144.8 2.8 collective-permute-start.14
  147.6 3.0 collective-permute-start.15
  151.7 2.8 collective-permute-start.6
  154.5 3.0 collective-permute-start.7
  168.4 7.7 %copy.46 = f32[256,27,256]{2,1,0:T(8,128)} copy(f32[256,27,256]{2,0,1:T(8,128)S(1)} %broadcast_multiply_fusion) | data formatting | bytes 14155776 | tf_op jit(solution)/shard_map/mul | solution.py:103
  176.1 8.5 %mul.17 = f32[6912,256]{1,0:T(8,128)} reshape(f32[256,27,256]{2,1,0:T(8,128)} %copy.46) | data formatting | bytes 14155776 | tf_op jit(solution)/shard_map/mul | solution.py:103
  184.6 293.5 %fusion.179 = (f32[56,256]{1,0:T(8,128)}, f32[56,256]{1,0:T(8,128)}) fusion(f32[6912,256]{1,0:T(8,128)} %mul.15, f32[6912,256]{1,0:T(8,128)} %mul.17), kind=kCustom, calls=%all-reduce-scatter.2 | all-reduce-scatter fusion | flops 3670017 | bytes 14270464
  479.5 4.4 collective-permute-start.21
  483.9 8.0 %collective-permute-start.22 = (f32[56,256]{1,0:T(8,128)}, f32[56,256]{1,0:T(8,128)}, u32[]{:S(2)}, u32[]{:S(2)}) collective-permute-start(f32[56,256]{1,0:T(8,128)} %get-tuple-element.15), channel_id=1, source_target_pairs={{0,2},{1,3},{2,4},{3,5},{4,6},{5,7},{6,8},{7,9},{8,10},{9,11},{10,... | collective-permute-start | bytes 172040
  491.9 10.9 %collective-permute-start.23 = (f32[56,256]{1,0:T(8,128)}, f32[56,256]{1,0:T(8,128)}, u32[]{:S(2)}, u32[]{:S(2)}) collective-permute-start(f32[56,256]{1,0:T(8,128)} %get-tuple-element.15), channel_id=1, source_target_pairs={{0,3},{1,4},{2,5},{3,6},{4,7},{5,8},{6,9},{7,10},{8,11},{9,12},{10... | collective-permute-start | bytes 172040
  502.9 11.3 %collective-permute-start.24 = (f32[56,256]{1,0:T(8,128)}, f32[56,256]{1,0:T(8,128)}, u32[]{:S(2)}, u32[]{:S(2)}) collective-permute-start(f32[56,256]{1,0:T(8,128)} %get-tuple-element.15), channel_id=1, source_target_pairs={{0,4},{1,5},{2,6},{3,7},{4,8},{5,9},{6,10},{7,11},{8,12},{9,13},{1... | collective-permute-start | bytes 172040
  514.2 17.1 %collective-permute-start.25 = (f32[30,256]{1,0:T(8,128)}, f32[30,256]{1,0:T(8,128)}, u32[]{:S(2)}, u32[]{:S(2)}) collective-permute-start(f32[30,256]{1,0:T(8,128)} %slice.943), channel_id=1, source_target_pairs={{0,5},{1,6},{2,7},{3,8},{4,9},{5,10},{6,11},{7,12},{8,13},{9,14},{... | collective-permute-start | bytes 92168
  531.7 2.5 fusion.180
  534.2 1.8 reshape.501
  536.0 1.8 reshape.502
  537.8 1.8 reshape.503
  539.6 1.8 reshape.504
  541.4 1.8 reshape.505
  543.2 1.8 reshape.506
  545.0 1.8 reshape.507
  546.7 1.8 reshape.508
  556.2 1.8 reshape.513
  558.0 1.8 reshape.515
  560.6 1.8 reshape.518
  576.8 3.1 collective-permute-start.16
  579.9 8.7 %collective-permute-start.17 = (f32[56,256]{1,0:T(8,128)S(1)}, f32[56,256]{1,0:T(8,128)S(1)}, u32[]{:S(2)}, u32[]{:S(2)}) collective-permute-start(f32[56,256]{1,0:T(8,128)S(1)} %copy-done.41), channel_id=1, source_target_pairs={{0,2},{1,3},{2,4},{3,5},{4,6},{5,7},{6,8},{7,9},{8,10},{9,11},{10,... | collective-permute-start | bytes 172040
  588.7 8.2 %collective-permute-start.18 = (f32[56,256]{1,0:T(8,128)S(1)}, f32[56,256]{1,0:T(8,128)S(1)}, u32[]{:S(2)}, u32[]{:S(2)}) collective-permute-start(f32[56,256]{1,0:T(8,128)S(1)} %copy-done.41), channel_id=1, source_target_pairs={{0,3},{1,4},{2,5},{3,6},{4,7},{5,8},{6,9},{7,10},{8,11},{9,12},{10... | collective-permute-start | bytes 172040
  596.9 14.2 %collective-permute-start.19 = (f32[56,256]{1,0:T(8,128)S(1)}, f32[56,256]{1,0:T(8,128)S(1)}, u32[]{:S(2)}, u32[]{:S(2)}) collective-permute-start(f32[56,256]{1,0:T(8,128)S(1)} %copy-done.41), channel_id=1, source_target_pairs={{0,4},{1,5},{2,6},{3,7},{4,8},{5,9},{6,10},{7,11},{8,12},{9,13},{1... | collective-permute-start | bytes 172040
  611.1 14.3 %collective-permute-start.20 = (f32[30,256]{1,0:T(8,128)}, f32[30,256]{1,0:T(8,128)S(1)}, u32[]{:S(2)}, u32[]{:S(2)}) collective-permute-start(f32[30,256]{1,0:T(8,128)} %slice.942), channel_id=1, source_target_pairs={{0,5},{1,6},{2,7},{3,8},{4,9},{5,10},{6,11},{7,12},{8,13},{9,14},{... | collective-permute-start | bytes 92168
  625.5 5.1 concatenate.113
  631.6 3.9 all-to-all-start.1
  640.7 8.3 %all-to-all-done.1 = f32[16,54,256]{2,1,0:T(8,128)S(1)} async-done(((f32[16,54,256]{2,1,0:T(8,128)}), f32[16,54,256]{2,1,0:T(8,128)S(1)}, u32[]{:S(2)}, u32[]{:S(2)}) %all-to-all-start.1) | async-done | bytes 884768 | tf_op jit(solution)/shard_map/all_to_all | solution.py:73
  649.9 5.2 all-to-all-start
  657.5 1.8 reshape.526
  665.5 3.1 all-to-all-done
  (316 shorter events, 106.6 us)
Async XLA Ops:
  7.2 68.9 %all-gather.3.cloned.1.call-start = ((), (), s32[]{:S(2)}) async-start(), calls=%async_computation.2 | async-start | bytes 3981312 | tf_op jit(solution)/shard_map/all_gather | solution.py:94
  7.9 556.0 %all-gather.5.cloned.1.call-start = ((), (), s32[]{:S(2)}) async-start(), calls=%async_computation.3 | async-start | bytes 3981312 | tf_op jit(solution)/shard_map/all_gather | solution.py:105
  9.1 11.4 %collective-permute-start = (bf16[1,4,1,12,256]{4,3,2,1,0:T(8,128)(2,1)S(1)}, bf16[1,4,1,12,256]{4,3,2,1,0:T(8,128)(2,1)S(1)}, u32[]{:S(2)}, u32[]{:S(2)}) collective-permute-start(bf16[1,4,1,12,256]{4,3,2,1,0:T(8,128)(2,1)S(1)} %get-tuple-element.88), channel_id=1, source_target_pairs={{0,4},{4,8},{8,12},{1,5},{5,9},{9,13},{2,6},{6,10},{10,14},{3,7},{... | collective-permute-start | bytes 73736 | tf_op jit(solution)/shard_map/ppermute | solution.py:13
  10.9 9.6 %collective-permute-start.1 = (bf16[1,4,1,12,256]{4,3,2,1,0:T(8,128)(2,1)S(1)}, bf16[1,4,1,12,256]{4,3,2,1,0:T(8,128)(2,1)S(1)}, u32[]{:S(2)}, u32[]{:S(2)}) collective-permute-start(bf16[1,4,1,12,256]{4,3,2,1,0:T(8,128)(2,1)S(1)} %get-tuple-element.89), channel_id=1, source_target_pairs={{4,0},{8,4},{12,8},{5,1},{9,5},{13,9},{6,2},{10,6},{14,10},{7,3},{... | collective-permute-start | bytes 73736 | tf_op jit(solution)/shard_map/ppermute | solution.py:16
  14.0 12.5 %collective-permute-start.8 = (bf16[1,4,1,12,256]{4,3,2,1,0:T(8,128)(2,1)S(1)}, bf16[1,4,1,12,256]{4,3,2,1,0:T(8,128)(2,1)S(1)}, u32[]{:S(2)}, u32[]{:S(2)}) collective-permute-start(bf16[1,4,1,12,256]{4,3,2,1,0:T(8,128)(2,1)S(1)} %get-tuple-element.81), channel_id=1, source_target_pairs={{0,4},{4,8},{8,12},{1,5},{5,9},{9,13},{2,6},{6,10},{10,14},{3,7},{... | collective-permute-start | bytes 73736 | tf_op jit(solution)/shard_map/ppermute | solution.py:13
  18.4 9.2 %collective-permute-start.9 = (bf16[1,4,1,12,256]{4,3,2,1,0:T(8,128)(2,1)S(1)}, bf16[1,4,1,12,256]{4,3,2,1,0:T(8,128)(2,1)S(1)}, u32[]{:S(2)}, u32[]{:S(2)}) collective-permute-start(bf16[1,4,1,12,256]{4,3,2,1,0:T(8,128)(2,1)S(1)} %get-tuple-element.80), channel_id=1, source_target_pairs={{4,0},{8,4},{12,8},{5,1},{9,5},{13,9},{6,2},{10,6},{14,10},{7,3},{... | collective-permute-start | bytes 73736 | tf_op jit(solution)/shard_map/ppermute | solution.py:16
  20.5 17.3 %copy-start.37 = (bf16[1,4,1,12,256]{4,3,2,1,0:T(8,128)(2,1)}, bf16[1,4,1,12,256]{4,3,2,1,0:T(8,128)(2,1)S(1)}, u32[]{:S(2)}) copy-start(bf16[1,4,1,12,256]{4,3,2,1,0:T(8,128)(2,1)S(1)} %collective-permute-done) | copy-start | bytes 73732
  20.5 17.3 %copy-start.39 = (bf16[1,4,1,12,256]{4,3,2,1,0:T(8,128)(2,1)}, bf16[1,4,1,12,256]{4,3,2,1,0:T(8,128)(2,1)S(1)}, u32[]{:S(2)}) copy-start(bf16[1,4,1,12,256]{4,3,2,1,0:T(8,128)(2,1)S(1)} %collective-permute-done.1) | copy-start | bytes 73732
  20.6 17.1 %collective-permute-start.2 = (bf16[1,4,14,1,256]{4,3,2,1,0:T(2,128)(2,1)S(1)}, bf16[1,4,14,1,256]{4,3,2,1,0:T(2,128)(2,1)S(1)}, u32[]{:S(2)}, u32[]{:S(2)}) collective-permute-start(bf16[1,4,14,1,256]{4,3,2,1,0:T(2,128)(2,1)S(1)} %get-tuple-element.77), channel_id=1, source_target_pairs={{0,1},{1,2},{2,3},{4,5},{5,6},{6,7},{8,9},{9,10},{10,11},{12,13},{... | collective-permute-start | bytes 86024 | tf_op jit(solution)/shard_map/ppermute | solution.py:13
  24.0 13.7 %collective-permute-start.3 = (bf16[1,4,14,1,256]{4,3,2,1,0:T(2,128)(2,1)S(1)}, bf16[1,4,14,1,256]{4,3,2,1,0:T(2,128)(2,1)S(1)}, u32[]{:S(2)}, u32[]{:S(2)}) collective-permute-start(bf16[1,4,14,1,256]{4,3,2,1,0:T(2,128)(2,1)S(1)} %get-tuple-element.76), channel_id=1, source_target_pairs={{1,0},{2,1},{3,2},{5,4},{6,5},{7,6},{9,8},{10,9},{11,10},{13,12},{... | collective-permute-start | bytes 86024 | tf_op jit(solution)/shard_map/ppermute | solution.py:16
  31.3 42.5 %collective-permute-start.10 = (bf16[1,4,14,1,256]{4,3,2,1,0:T(2,128)(2,1)}, bf16[1,4,14,1,256]{4,3,2,1,0:T(2,128)(2,1)}, u32[]{:S(2)}, u32[]{:S(2)}) collective-permute-start(bf16[1,4,14,1,256]{4,3,2,1,0:T(2,128)(2,1)} %get-tuple-element.56), channel_id=1, source_target_pairs={{0,1},{1,2},{2,3},{4,5},{5,6},{6,7},{8,9},{9,10},{10,11},{12,13},{... | collective-permute-start | bytes 86024 | tf_op jit(solution)/shard_map/ppermute | solution.py:13
  34.7 39.1 %collective-permute-start.11 = (bf16[1,4,14,1,256]{4,3,2,1,0:T(2,128)(2,1)}, bf16[1,4,14,1,256]{4,3,2,1,0:T(2,128)(2,1)}, u32[]{:S(2)}, u32[]{:S(2)}) collective-permute-start(bf16[1,4,14,1,256]{4,3,2,1,0:T(2,128)(2,1)} %get-tuple-element.57), channel_id=1, source_target_pairs={{1,0},{2,1},{3,2},{5,4},{6,5},{7,6},{9,8},{10,9},{11,10},{13,12},{... | collective-permute-start | bytes 86024 | tf_op jit(solution)/shard_map/ppermute | solution.py:16
  39.4 2.4 copy-start.38
  39.4 2.4 copy-start.40
  39.4 2.4 copy-start.46
  73.7 8.9 %copy-start.18 = (bf16[576,256]{1,0:T(8,128)(2,1)S(1)}, bf16[576,256]{1,0:T(8,128)(2,1)}, u32[]{:S(2)}) copy-start(bf16[576,256]{1,0:T(8,128)(2,1)} %reshape.476) | copy-start | bytes 884740
  76.0 7.8 %copy-start.1 = (bf16[256,27,256]{2,0,1:T(8,128)(2,1)S(1)}, bf16[256,27,256]{2,0,1:T(8,128)(2,1)}, u32[]{:S(2)}) copy-start(bf16[256,27,256]{2,0,1:T(8,128)(2,1)} %all-gather.3.cloned.1.call-done) | copy-start | bytes 10616836
  76.0 7.8 %copy-start.16 = (bf16[576,256]{1,0:T(8,128)(2,1)S(1)}, bf16[576,256]{1,0:T(8,128)(2,1)}, u32[]{:S(2)}) copy-start(bf16[576,256]{1,0:T(8,128)(2,1)} %reshape.477) | copy-start | bytes 884740
  76.0 12.0 %copy-start.15 = (bf16[576,256]{1,0:T(8,128)(2,1)S(1)}, bf16[576,256]{1,0:T(8,128)(2,1)}, u32[]{:S(2)}) copy-start(bf16[576,256]{1,0:T(8,128)(2,1)} %reshape.481) | copy-start | bytes 884740
  78.7 9.6 %copy-start.14 = (bf16[576,256]{1,0:T(8,128)(2,1)S(1)}, bf16[576,256]{1,0:T(8,128)(2,1)}, u32[]{:S(2)}) copy-start(bf16[576,256]{1,0:T(8,128)(2,1)} %reshape.482) | copy-start | bytes 884740
  80.0 8.6 %copy-start.5 = (bf16[576,256]{1,0:T(8,128)(2,1)S(1)}, bf16[576,256]{1,0:T(8,128)(2,1)}, u32[]{:S(2)}) copy-start(bf16[576,256]{1,0:T(8,128)(2,1)} %reshape.483) | copy-start | bytes 884740
  82.6 6.3 copy-start.13
  83.9 5.3 copy-start.8
  84.2 5.3 copy-start.12
  85.5 4.3 copy-start.11
  86.7 3.3 copy-start.4
  91.7 8.7 %copy-start.31 = (bf16[1,6,14,14,256]{4,3,2,1,0:T(8,128)(2,1)S(1)}, bf16[1,6,14,14,256]{4,3,2,1,0:T(8,128)(2,1)}, u32[]{:S(2)}) copy-start(bf16[1,6,14,14,256]{4,3,2,1,0:T(8,128)(2,1)} %select_maximum_fusion.4) | copy-start | bytes 1806340
  94.1 50.6 %collective-permute-start.12 = (bf16[1,4,1,12,256]{4,3,2,1,0:T(8,128)(2,1)S(1)}, bf16[1,4,1,12,256]{4,3,2,1,0:T(8,128)(2,1)S(1)}, u32[]{:S(2)}, u32[]{:S(2)}) collective-permute-start(bf16[1,4,1,12,256]{4,3,2,1,0:T(8,128)(2,1)S(1)} %get-tuple-element.78), channel_id=1, source_target_pairs={{0,4},{4,8},{8,12},{1,5},{5,9},{9,13},{2,6},{6,10},{10,14},{3,7},{... | collective-permute-start | bytes 73736 | tf_op jit(solution)/shard_map/ppermute | solution.py:13
  97.3 47.3 %collective-permute-start.13 = (bf16[1,4,1,12,256]{4,3,2,1,0:T(8,128)(2,1)S(1)}, bf16[1,4,1,12,256]{4,3,2,1,0:T(8,128)(2,1)S(1)}, u32[]{:S(2)}, u32[]{:S(2)}) collective-permute-start(bf16[1,4,1,12,256]{4,3,2,1,0:T(8,128)(2,1)S(1)} %get-tuple-element.79), channel_id=1, source_target_pairs={{4,0},{8,4},{12,8},{5,1},{9,5},{13,9},{6,2},{10,6},{14,10},{7,3},{... | collective-permute-start | bytes 73736 | tf_op jit(solution)/shard_map/ppermute | solution.py:16
  105.0 2.5 copy-start.6
  107.4 2.7 copy-start.50
  138.1 12.6 %collective-permute-start.4 = (bf16[1,4,1,12,256]{4,3,2,1,0:T(8,128)(2,1)S(1)}, bf16[1,4,1,12,256]{4,3,2,1,0:T(8,128)(2,1)S(1)}, u32[]{:S(2)}, u32[]{:S(2)}) collective-permute-start(bf16[1,4,1,12,256]{4,3,2,1,0:T(8,128)(2,1)S(1)} %get-tuple-element.84), channel_id=1, source_target_pairs={{0,4},{4,8},{8,12},{1,5},{5,9},{9,13},{2,6},{6,10},{10,14},{3,7},{... | collective-permute-start | bytes 73736 | tf_op jit(solution)/shard_map/ppermute | solution.py:13
  143.4 7.3 %collective-permute-start.5 = (bf16[1,4,1,12,256]{4,3,2,1,0:T(8,128)(2,1)S(1)}, bf16[1,4,1,12,256]{4,3,2,1,0:T(8,128)(2,1)S(1)}, u32[]{:S(2)}, u32[]{:S(2)}) collective-permute-start(bf16[1,4,1,12,256]{4,3,2,1,0:T(8,128)(2,1)S(1)} %get-tuple-element.85), channel_id=1, source_target_pairs={{4,0},{8,4},{12,8},{5,1},{9,5},{13,9},{6,2},{10,6},{14,10},{7,3},{... | collective-permute-start | bytes 73736 | tf_op jit(solution)/shard_map/ppermute | solution.py:16
  144.8 12.8 %collective-permute-start.14 = (bf16[1,4,14,1,256]{4,3,2,1,0:T(2,128)(2,1)S(1)}, bf16[1,4,14,1,256]{4,3,2,1,0:T(2,128)(2,1)S(1)}, u32[]{:S(2)}, u32[]{:S(2)}) collective-permute-start(bf16[1,4,14,1,256]{4,3,2,1,0:T(2,128)(2,1)S(1)} %get-tuple-element.54), channel_id=1, source_target_pairs={{0,1},{1,2},{2,3},{4,5},{5,6},{6,7},{8,9},{9,10},{10,11},{12,13},{... | collective-permute-start | bytes 86024 | tf_op jit(solution)/shard_map/ppermute | solution.py:13
  147.6 9.9 %collective-permute-start.15 = (bf16[1,4,14,1,256]{4,3,2,1,0:T(2,128)(2,1)S(1)}, bf16[1,4,14,1,256]{4,3,2,1,0:T(2,128)(2,1)S(1)}, u32[]{:S(2)}, u32[]{:S(2)}) collective-permute-start(bf16[1,4,14,1,256]{4,3,2,1,0:T(2,128)(2,1)S(1)} %get-tuple-element.55), channel_id=1, source_target_pairs={{1,0},{2,1},{3,2},{5,4},{6,5},{7,6},{9,8},{10,9},{11,10},{13,12},{... | collective-permute-start | bytes 86024 | tf_op jit(solution)/shard_map/ppermute | solution.py:16
  150.7 380.7 %copy-start.34 = (bf16[1,4,1,12,256]{4,3,2,1,0:T(8,128)(2,1)}, bf16[1,4,1,12,256]{4,3,2,1,0:T(8,128)(2,1)S(1)}, u32[]{:S(2)}) copy-start(bf16[1,4,1,12,256]{4,3,2,1,0:T(8,128)(2,1)S(1)} %collective-permute-done.4) | copy-start | bytes 73732
  150.7 380.7 %copy-start.36 = (bf16[1,4,1,12,256]{4,3,2,1,0:T(8,128)(2,1)}, bf16[1,4,1,12,256]{4,3,2,1,0:T(8,128)(2,1)S(1)}, u32[]{:S(2)}) copy-start(bf16[1,4,1,12,256]{4,3,2,1,0:T(8,128)(2,1)S(1)} %collective-permute-done.5) | copy-start | bytes 73732
  151.7 351.2 %collective-permute-start.6 = (bf16[1,4,14,1,256]{4,3,2,1,0:T(2,128)(2,1)S(1)}, bf16[1,4,14,1,256]{4,3,2,1,0:T(2,128)(2,1)S(1)}, u32[]{:S(2)}, u32[]{:S(2)}) collective-permute-start(bf16[1,4,14,1,256]{4,3,2,1,0:T(2,128)(2,1)S(1)} %get-tuple-element.67), channel_id=1, source_target_pairs={{0,1},{1,2},{2,3},{4,5},{5,6},{6,7},{8,9},{9,10},{10,11},{12,13},{... | collective-permute-start | bytes 86024 | tf_op jit(solution)/shard_map/ppermute | solution.py:13
  154.5 359.7 %collective-permute-start.7 = (bf16[1,4,14,1,256]{4,3,2,1,0:T(2,128)(2,1)S(1)}, bf16[1,4,14,1,256]{4,3,2,1,0:T(2,128)(2,1)S(1)}, u32[]{:S(2)}, u32[]{:S(2)}) collective-permute-start(bf16[1,4,14,1,256]{4,3,2,1,0:T(2,128)(2,1)S(1)} %get-tuple-element.66), channel_id=1, source_target_pairs={{1,0},{2,1},{3,2},{5,4},{6,5},{7,6},{9,8},{10,9},{11,10},{13,12},{... | collective-permute-start | bytes 86024 | tf_op jit(solution)/shard_map/ppermute | solution.py:16
  479.5 100.5 %collective-permute-start.21 = (f32[56,256]{1,0:T(8,128)}, f32[56,256]{1,0:T(8,128)}, u32[]{:S(2)}, u32[]{:S(2)}) collective-permute-start(f32[56,256]{1,0:T(8,128)} %get-tuple-element.15), channel_id=1, source_target_pairs={{0,1},{1,2},{2,3},{3,4},{4,5},{5,6},{6,7},{7,8},{8,9},{9,10},{10,1... | collective-permute-start | bytes 172040
  483.9 104.8 %collective-permute-start.22 = (f32[56,256]{1,0:T(8,128)}, f32[56,256]{1,0:T(8,128)}, u32[]{:S(2)}, u32[]{:S(2)}) collective-permute-start(f32[56,256]{1,0:T(8,128)} %get-tuple-element.15), channel_id=1, source_target_pairs={{0,2},{1,3},{2,4},{3,5},{4,6},{5,7},{6,8},{7,9},{8,10},{9,11},{10,... | collective-permute-start | bytes 172040
  491.9 105.0 %collective-permute-start.23 = (f32[56,256]{1,0:T(8,128)}, f32[56,256]{1,0:T(8,128)}, u32[]{:S(2)}, u32[]{:S(2)}) collective-permute-start(f32[56,256]{1,0:T(8,128)} %get-tuple-element.15), channel_id=1, source_target_pairs={{0,3},{1,4},{2,5},{3,6},{4,7},{5,8},{6,9},{7,10},{8,11},{9,12},{10... | collective-permute-start | bytes 172040
  502.8 28.5 %copy-start.43 = (bf16[1,4,14,1,256]{4,3,2,1,0:T(2,128)(2,1)}, bf16[1,4,14,1,256]{4,3,2,1,0:T(2,128)(2,1)S(1)}, u32[]{:S(2)}) copy-start(bf16[1,4,14,1,256]{4,3,2,1,0:T(2,128)(2,1)S(1)} %collective-permute-done.6) | copy-start | bytes 86020
  502.9 108.2 %collective-permute-start.24 = (f32[56,256]{1,0:T(8,128)}, f32[56,256]{1,0:T(8,128)}, u32[]{:S(2)}, u32[]{:S(2)}) collective-permute-start(f32[56,256]{1,0:T(8,128)} %get-tuple-element.15), channel_id=1, source_target_pairs={{0,4},{1,5},{2,6},{3,7},{4,8},{5,9},{6,10},{7,11},{8,12},{9,13},{1... | collective-permute-start | bytes 172040
  514.2 17.2 %copy-start.44 = (bf16[1,4,14,1,256]{4,3,2,1,0:T(2,128)(2,1)}, bf16[1,4,14,1,256]{4,3,2,1,0:T(2,128)(2,1)S(1)}, u32[]{:S(2)}) copy-start(bf16[1,4,14,1,256]{4,3,2,1,0:T(2,128)(2,1)S(1)} %collective-permute-done.7) | copy-start | bytes 86020
  514.2 62.6 %collective-permute-start.25 = (f32[30,256]{1,0:T(8,128)}, f32[30,256]{1,0:T(8,128)}, u32[]{:S(2)}, u32[]{:S(2)}) collective-permute-start(f32[30,256]{1,0:T(8,128)} %slice.943), channel_id=1, source_target_pairs={{0,5},{1,6},{2,7},{3,8},{4,9},{5,10},{6,11},{7,12},{8,13},{9,14},{... | collective-permute-start | bytes 92168
  531.7 17.6 %copy-start.35 = (bf16[1,4,1,12,256]{4,3,2,1,0:T(8,128)(2,1)S(1)}, bf16[1,4,1,12,256]{4,3,2,1,0:T(8,128)(2,1)}, u32[]{:S(2)}) copy-start(bf16[1,4,1,12,256]{4,3,2,1,0:T(8,128)(2,1)} %copy-done.34) | copy-start | bytes 73732
  559.8 12.7 %copy-start.20 = (bf16[576,256]{1,0:T(8,128)(2,1)S(1)}, bf16[576,256]{1,0:T(8,128)(2,1)}, u32[]{:S(2)}) copy-start(bf16[576,256]{1,0:T(8,128)(2,1)} %reshape.507) | copy-start | bytes 884740
  562.4 10.4 %copy-start.19 = (bf16[576,256]{1,0:T(8,128)(2,1)S(1)}, bf16[576,256]{1,0:T(8,128)(2,1)}, u32[]{:S(2)}) copy-start(bf16[576,256]{1,0:T(8,128)(2,1)} %reshape.508) | copy-start | bytes 884740
  563.1 9.0 %copy-start.21 = (bf16[576,256]{1,0:T(8,128)(2,1)S(1)}, bf16[576,256]{1,0:T(8,128)(2,1)}, u32[]{:S(2)}) copy-start(bf16[576,256]{1,0:T(8,128)(2,1)} %reshape.506) | copy-start | bytes 884740
  563.9 9.1 %copy-start.17 = (bf16[576,256]{1,0:T(8,128)(2,1)S(1)}, bf16[576,256]{1,0:T(8,128)(2,1)}, u32[]{:S(2)}) copy-start(bf16[576,256]{1,0:T(8,128)(2,1)} %reshape.509) | copy-start | bytes 884740
  563.9 7.9 %copy-start = (bf16[256,27,256]{2,0,1:T(8,128)(2,1)S(1)}, bf16[256,27,256]{2,0,1:T(8,128)(2,1)}, u32[]{:S(2)}) copy-start(bf16[256,27,256]{2,0,1:T(8,128)(2,1)} %all-gather.5.cloned.1.call-done) | copy-start | bytes 10616836
  564.0 7.9 %copy-start.22 = (bf16[576,256]{1,0:T(8,128)(2,1)S(1)}, bf16[576,256]{1,0:T(8,128)(2,1)}, u32[]{:S(2)}) copy-start(bf16[576,256]{1,0:T(8,128)(2,1)} %reshape.505) | copy-start | bytes 884740
  566.6 6.7 copy-start.27
  567.9 5.7 copy-start.3
  570.5 3.4 copy-start.28
  576.8 63.1 %collective-permute-start.16 = (f32[56,256]{1,0:T(8,128)S(1)}, f32[56,256]{1,0:T(8,128)S(1)}, u32[]{:S(2)}, u32[]{:S(2)}) collective-permute-start(f32[56,256]{1,0:T(8,128)S(1)} %copy-done.41), channel_id=1, source_target_pairs={{0,1},{1,2},{2,3},{3,4},{4,5},{5,6},{6,7},{7,8},{8,9},{9,10},{10,1... | collective-permute-start | bytes 172040
  579.9 59.9 %collective-permute-start.17 = (f32[56,256]{1,0:T(8,128)S(1)}, f32[56,256]{1,0:T(8,128)S(1)}, u32[]{:S(2)}, u32[]{:S(2)}) collective-permute-start(f32[56,256]{1,0:T(8,128)S(1)} %copy-done.41), channel_id=1, source_target_pairs={{0,2},{1,3},{2,4},{3,5},{4,6},{5,7},{6,8},{7,9},{8,10},{9,11},{10,... | collective-permute-start | bytes 172040
  588.7 51.2 %collective-permute-start.18 = (f32[56,256]{1,0:T(8,128)S(1)}, f32[56,256]{1,0:T(8,128)S(1)}, u32[]{:S(2)}, u32[]{:S(2)}) collective-permute-start(f32[56,256]{1,0:T(8,128)S(1)} %copy-done.41), channel_id=1, source_target_pairs={{0,3},{1,4},{2,5},{3,6},{4,7},{5,8},{6,9},{7,10},{8,11},{9,12},{10... | collective-permute-start | bytes 172040
  596.9 43.0 %collective-permute-start.19 = (f32[56,256]{1,0:T(8,128)S(1)}, f32[56,256]{1,0:T(8,128)S(1)}, u32[]{:S(2)}, u32[]{:S(2)}) collective-permute-start(f32[56,256]{1,0:T(8,128)S(1)} %copy-done.41), channel_id=1, source_target_pairs={{0,4},{1,5},{2,6},{3,7},{4,8},{5,9},{6,10},{7,11},{8,12},{9,13},{1... | collective-permute-start | bytes 172040
  611.1 28.7 %collective-permute-start.20 = (f32[30,256]{1,0:T(8,128)}, f32[30,256]{1,0:T(8,128)S(1)}, u32[]{:S(2)}, u32[]{:S(2)}) collective-permute-start(f32[30,256]{1,0:T(8,128)} %slice.942), channel_id=1, source_target_pairs={{0,5},{1,6},{2,7},{3,8},{4,9},{5,10},{6,11},{7,12},{8,13},{9,14},{... | collective-permute-start | bytes 92168
  631.6 27.7 %copy-start.2 = (bf16[1,4,12,12,256]{4,3,2,1,0:T(8,128)(2,1)S(1)}, bf16[1,4,12,12,256]{4,3,2,1,0:T(8,128)(2,1)}, u32[]{:S(2)}) copy-start(bf16[1,4,12,12,256]{4,3,2,1,0:T(8,128)(2,1)} %get-tuple-element.16) | copy-start | bytes 884740
  631.6 17.4 %all-to-all-start.1 = ((f32[16,54,256]{2,1,0:T(8,128)}), f32[16,54,256]{2,1,0:T(8,128)S(1)}, u32[]{:S(2)}, u32[]{:S(2)}) async-start(f32[16,54,256]{2,1,0:T(8,128)} %stack.263), calls=%async_computation.1 | async-start | bytes 1835008 | tf_op jit(solution)/shard_map/all_to_all | solution.py:73
  649.9 18.7 %all-to-all-start = ((f32[16,54,256]{2,1,0:T(8,128)}), f32[16,54,256]{2,1,0:T(8,128)S(1)}, u32[]{:S(2)}, u32[]{:S(2)}) async-start(f32[16,54,256]{2,1,0:T(8,128)} %stack.234), calls=%async_computation | async-start | bytes 1835008 | tf_op jit(solution)/shard_map/all_to_all | solution.py:73
  (19 other events, 31.0 us)
Sparse Core Ops, SparseCore 0:
  10.3 63.1 all-gather.2
  75.9 64.0 all-gather.4
